TPU v7x, 32 devices: a whole 2x2x4 slice. The times are simulated.
32 devices in a mesh: wide: 8 (over z, y), narrow: 4 (over x, core).
Axes of the slice: x: 2, y: 2, z: 4, core: 2. Of those that a mesh axis runs over, the one named last changes fastest.
Arguments:
- media_feats: bfloat16 [8, 2048, 1536], P('wide', 'narrow'), may hold values from -6 to 6
- latents: bfloat16 [8, 64, 1536], P('wide', 'narrow'), may hold values from -6 to 6
- frame_counts: int32 [8], P('wide'), may hold values from 1 to 8, as said below
- media_mask: int32 [8, 2048], P('wide'), may hold values 0 or 1
- time_embed: bfloat16 [8, 1536], replicated, may hold values from -3 to 3
- media_gain: float32 [1536], replicated, may hold values from 0.1 to 1.9
- media_bias: float32 [1536], replicated, may hold values from -1.75 to 1.75
- latent_gain: float32 [1536], replicated, may hold values from 0.1 to 1.9
- latent_bias: float32 [1536], replicated, may hold values from -1.75 to 1.75
- ffn_gain: float32 [1536], replicated, may hold values from 0.1 to 1.9
- ffn_bias: float32 [1536], replicated, may hold values from -1.75 to 1.75
- query_weight: bfloat16 [1536, 1536], P('wide', 'narrow'), may hold values from -0.3125 to 0.3125
- keyval_weight: bfloat16 [1536, 2, 1536], P('wide', None, 'narrow'), may hold values from -0.15625 to 0.15625
- output_weight: bfloat16 [1536, 1536], P('narrow', 'wide'), may hold values from -0.625 to 0.625
- up_weight: bfloat16 [1536, 6144], P(None, 'narrow'), may hold values from -0.15625 to 0.15625
- down_weight: bfloat16 [6144, 1536], P('narrow'), may hold values from -0.078125 to 0.078125
- cotangent: bfloat16 [8, 64, 1536], P('wide', 'narrow'), may hold values from -6 to 6
Outputs:
- out_latents: bfloat16 [8, 64, 1536], P('wide', 'narrow')
- grad_media: bfloat16 [8, 2048, 1536], P('wide', 'narrow')
- grad_latents: bfloat16 [8, 64, 1536], P('wide', 'narrow')
- grad_time_embed: float32 [8, 1536], P(None, ('wide', 'narrow'))
- grad_media_gain: float32 [1536], P(('wide', 'narrow'))
- grad_media_bias: float32 [1536], P(('wide', 'narrow'))
- grad_latent_gain: float32 [1536], P(('wide', 'narrow'))
- grad_latent_bias: float32 [1536], P(('wide', 'narrow'))
- grad_ffn_gain: float32 [1536], P(('wide', 'narrow'))
- grad_ffn_bias: float32 [1536], P(('wide', 'narrow'))
- grad_query_weight: float32 [1536, 1536], P('wide', 'narrow')
- grad_keyval_weight: float32 [1536, 2, 1536], P('wide', None, 'narrow')
- grad_output_weight: float32 [1536, 1536], P('narrow', 'wide')
- grad_up_weight: float32 [1536, 6144], P('wide', 'narrow')
- grad_down_weight: float32 [6144, 1536], P('narrow', 'wide')
Inputs may be any that keep to these rules, and one draw needn't show every extreme that they name: `frame_counts`: frames of each item; some item has exactly 8.
All inputs are finite; a program needn't handle non-finite values. No bound on the sum of `media_mask` on one device may be relied on, other than what follows from the above.
Results may differ from a plain program's by a relative error of at most 0.02.
Values may be sent and summed in bfloat16 or wider, within the bound.
A program may use at most 128 MiB of HBM per device.

v0:
```python
import math
import jax
import jax.numpy as jnp
from jax import lax
from jax.sharding import PartitionSpec as P

HEADS = 16
HEAD_DIM = 96
FRAMES_MAX = 8
PATCHES = 256
EPS = 1e-05
ENT_COEF = 4.0
HIGH = lax.Precision.HIGHEST


def norm_forward(values, norm_gain, norm_bias):
    row_mean = jnp.mean(values, axis=-1, keepdims=True)
    centered = values - row_mean
    inv_std = lax.rsqrt(jnp.mean(centered * centered, axis=-1, keepdims=True) + EPS)
    normed = centered * inv_std
    return (normed * norm_gain + norm_bias, normed, inv_std)


def norm_backward(grad_out, normed, inv_std, norm_gain):
    scaled = grad_out * norm_gain
    grad_in = inv_std * (
        scaled
        - jnp.mean(scaled, axis=-1, keepdims=True)
        - normed * jnp.mean(scaled * normed, axis=-1, keepdims=True)
    )
    return (grad_in, jnp.sum(grad_out * normed, axis=0), jnp.sum(grad_out, axis=0))


def gelu_slope(pre_act):
    cdf_part = 0.5 * (1.0 + lax.erf(pre_act * (1.0 / math.sqrt(2.0))))
    density = jnp.exp(-0.5 * pre_act * pre_act) * (1.0 / math.sqrt(2.0 * math.pi))
    return cdf_part + pre_act * density


def body(
    media_feats,
    latents,
    frame_counts,
    media_mask,
    time_embed,
    media_gain,
    media_bias,
    latent_gain,
    latent_bias,
    ffn_gain,
    ffn_bias,
    query_weight,
    keyval_weight,
    output_weight,
    up_weight,
    down_weight,
    cotangent,
):
    item_count = media_feats.shape[0]
    own_media = media_feats.shape[1]
    width = media_feats.shape[2]
    own_latent = latents.shape[1]
    narrow_size = lax.axis_size("narrow")
    narrow_pos = lax.axis_index("narrow")
    media_total = own_media * narrow_size
    latent_total = own_latent * narrow_size
    head_local = HEADS // narrow_size
    cols = head_local * HEAD_DIM
    key_total = media_total + latent_total
    all_ids = jnp.arange(media_total, dtype=jnp.int32) // PATCHES
    valid_tok = (all_ids[None, :] < frame_counts[:, None]) & (media_mask > 0)
    local_count = jnp.sum(valid_tok.astype(jnp.float32)) + float(item_count * latent_total)
    total_count = lax.psum(local_count, "wide")
    all_items = item_count * lax.axis_size("wide")
    ent_weight = ENT_COEF * float(all_items * media_total) / total_count
    query_own, keyval_own, output_own = (
        lax.all_gather(query_weight, "wide", axis=0, tiled=True),
        lax.all_gather(keyval_weight, "wide", axis=0, tiled=True),
        lax.all_gather(output_weight, "wide", axis=1, tiled=True),
    )
    query_full, keyval_full = (
        lax.all_gather(query_own, "narrow", axis=1, tiled=True),
        lax.all_gather(keyval_own, "narrow", axis=2, tiled=True),
    )
    keyval_flat = keyval_own.reshape(width, 2 * cols)
    own_ids = (narrow_pos * own_media + jnp.arange(own_media, dtype=jnp.int32)) // PATCHES
    frame_onehot = own_ids[:, None] == jnp.arange(FRAMES_MAX, dtype=jnp.int32)[None, :]
    time_rows = jnp.dot(
        frame_onehot.astype(jnp.bfloat16), time_embed, preferred_element_type=jnp.float32
    )
    score_scale = HEAD_DIM ** (-0.5)

    def item_step(carry, item):
        (
            down_acc,
            up_acc,
            output_acc,
            keyval_acc,
            query_acc,
            mg_acc,
            mb_acc,
            lg_acc,
            lb_acc,
            fg_acc,
            fb_acc,
            time_acc,
        ) = carry
        media_one, latent_one, valid_one, cot_one = item
        media_nf, media_hat, media_istd = norm_forward(
            media_one.astype(jnp.float32) + time_rows, media_gain, media_bias
        )
        latent_f32 = latent_one.astype(jnp.float32)
        latent_nf, latent_hat, latent_istd = norm_forward(latent_f32, latent_gain, latent_bias)
        media_all, latent_all = (
            lax.all_gather(media_nf.astype(jnp.bfloat16), "narrow", axis=0, tiled=True),
            lax.all_gather(latent_nf.astype(jnp.bfloat16), "narrow", axis=0, tiled=True),
        )
        keys_in = jnp.concatenate([media_all, latent_all], axis=0)
        query_act = jnp.dot(latent_all, query_own, preferred_element_type=jnp.float32).astype(
            jnp.bfloat16
        )
        key_vals = jnp.dot(keys_in, keyval_flat, preferred_element_type=jnp.float32).astype(
            jnp.bfloat16
        )
        query_heads = query_act.reshape(latent_total, head_local, HEAD_DIM)
        key_heads = key_vals[:, :cols].reshape(key_total, head_local, HEAD_DIM)
        value_heads = key_vals[:, cols:].reshape(key_total, head_local, HEAD_DIM)
        key_valid = jnp.concatenate([valid_one, jnp.ones((latent_total,), dtype=bool)])
        scores = (
            jnp.einsum("lhd,khd->hlk", query_heads, key_heads, preferred_element_type=jnp.float32)
            * score_scale
        )
        open_keys = key_valid[None, None, :]
        masked = jnp.where(open_keys, scores, -1e30)
        row_top = jnp.max(masked, axis=-1)
        expo = jnp.exp(masked - row_top[..., None])
        prob_all = expo / jnp.sum(expo, axis=-1)[..., None]
        prob_low = prob_all.astype(jnp.bfloat16)
        plain_scores = jnp.where(open_keys, scores, 0.0)
        mean_score = jnp.sum(prob_all * plain_scores, axis=-1)
        attn_out = jnp.einsum(
            "hlk,khd->lhd", prob_low, value_heads, preferred_element_type=jnp.float32
        ).reshape(latent_total, cols)
        attn_low = attn_out.astype(jnp.bfloat16)
        branch_part = jnp.dot(attn_low, output_own, preferred_element_type=jnp.float32)
        branch_own = lax.psum_scatter(
            branch_part.astype(jnp.bfloat16), "narrow", scatter_dimension=0, tiled=True
        ).astype(jnp.float32)
        latent_mid = latent_f32 + branch_own
        hidden_f, hidden_hat, hidden_istd = norm_forward(latent_mid, ffn_gain, ffn_bias)
        hidden_all, cot_all = (
            lax.all_gather(hidden_f.astype(jnp.bfloat16), "narrow", axis=0, tiled=True),
            lax.all_gather(cot_one, "narrow", axis=0, tiled=True),
        )
        pre_act = jnp.dot(hidden_all, up_weight, preferred_element_type=jnp.float32)
        act_low = jax.nn.gelu(pre_act, approximate=False).astype(jnp.bfloat16)
        ffn_part = jnp.dot(act_low, down_weight, preferred_element_type=jnp.float32)
        ffn_own = lax.psum_scatter(
            ffn_part.astype(jnp.bfloat16), "narrow", scatter_dimension=0, tiled=True
        ).astype(jnp.float32)
        out_one = (latent_mid + ffn_own).astype(jnp.bfloat16)
        down_acc = down_acc + jnp.einsum(
            "lf,ld->fd", act_low, cot_all, preferred_element_type=jnp.float32
        )
        grad_act = jnp.einsum("ld,fd->lf", cot_all, down_weight, preferred_element_type=jnp.float32)
        grad_pre = (grad_act * gelu_slope(pre_act)).astype(jnp.bfloat16)
        up_acc = up_acc + jnp.einsum(
            "ld,lf->df", hidden_all, grad_pre, preferred_element_type=jnp.float32
        )
        hidden_part = jnp.einsum(
            "lf,df->ld", grad_pre, up_weight, preferred_element_type=jnp.float32
        )
        grad_hidden = lax.psum_scatter(
            hidden_part.astype(jnp.bfloat16), "narrow", scatter_dimension=0, tiled=True
        ).astype(jnp.float32)
        grad_norm, fg_part, fb_part = norm_backward(grad_hidden, hidden_hat, hidden_istd, ffn_gain)
        grad_mid = cot_one.astype(jnp.float32) + grad_norm
        grad_branch_all = lax.all_gather(
            grad_mid.astype(jnp.bfloat16), "narrow", axis=0, tiled=True
        )
        output_acc = output_acc + jnp.einsum(
            "lc,ld->cd", attn_low, grad_branch_all, preferred_element_type=jnp.float32
        )
        grad_attn = jnp.einsum(
            "ld,cd->lc", grad_branch_all, output_own, preferred_element_type=jnp.float32
        ).astype(jnp.bfloat16)
        row_dots = jnp.sum(
            (grad_attn.astype(jnp.float32) * attn_out).reshape(latent_total, head_local, HEAD_DIM),
            axis=-1,
        )
        shift_rows = (jnp.transpose(row_dots, (1, 0)) - ent_weight * mean_score)[..., None]
        grad_heads = grad_attn.reshape(latent_total, head_local, HEAD_DIM)
        grad_prob = jnp.einsum(
            "lhd,khd->hlk", grad_heads, value_heads, preferred_element_type=jnp.float32
        )
        grad_scores = (prob_all * (grad_prob - ent_weight * plain_scores - shift_rows)).astype(
            jnp.bfloat16
        )
        grad_values = jnp.einsum(
            "hlk,lhd->khd", prob_low, grad_heads, preferred_element_type=jnp.float32
        ).reshape(key_total, cols)
        grad_keys = (
            jnp.einsum(
                "hlk,lhd->khd", grad_scores, query_heads, preferred_element_type=jnp.float32
            ).reshape(key_total, cols)
            * score_scale
        )
        grad_query = (
            jnp.einsum(
                "hlk,khd->lhd", grad_scores, key_heads, preferred_element_type=jnp.float32
            ).reshape(latent_total, cols)
            * score_scale
        ).astype(jnp.bfloat16)
        grad_pairs = jnp.concatenate([grad_keys, grad_values], axis=-1).astype(jnp.bfloat16)
        keyval_acc = keyval_acc + jnp.einsum(
            "kd,ke->de", keys_in, grad_pairs, preferred_element_type=jnp.float32
        )
        query_acc = query_acc + jnp.einsum(
            "ld,lc->dc", latent_all, grad_query, preferred_element_type=jnp.float32
        )
        media_pairs = grad_pairs[:media_total].reshape(media_total, 2, cols)
        latent_pairs = jnp.concatenate(
            [
                grad_pairs[media_total:].reshape(latent_total, 2, cols),
                grad_query.reshape(latent_total, 1, cols),
            ],
            axis=1,
        )
        media_back, latent_back = (
            lax.all_to_all(media_pairs, "narrow", split_axis=0, concat_axis=2, tiled=True),
            lax.all_to_all(latent_pairs, "narrow", split_axis=0, concat_axis=2, tiled=True),
        )
        grad_media_rows = jnp.einsum(
            "rsc,dsc->rd", media_back, keyval_full, preferred_element_type=jnp.float32
        )
        grad_latent_normed = jnp.einsum(
            "rsc,dsc->rd", latent_back[:, :2], keyval_full, preferred_element_type=jnp.float32
        ) + jnp.einsum(
            "rc,dc->rd", latent_back[:, 2], query_full, preferred_element_type=jnp.float32
        )
        grad_media_in, mg_part, mb_part = norm_backward(
            grad_media_rows, media_hat, media_istd, media_gain
        )
        time_acc = time_acc + jnp.einsum(
            "mf,md->fd", frame_onehot.astype(jnp.float32), grad_media_in, precision=HIGH
        )
        grad_latent_in, lg_part, lb_part = norm_backward(
            grad_latent_normed, latent_hat, latent_istd, latent_gain
        )
        grad_latent_one = (grad_mid + grad_latent_in).astype(jnp.bfloat16)
        carry = (
            down_acc,
            up_acc,
            output_acc,
            keyval_acc,
            query_acc,
            mg_acc + mg_part,
            mb_acc + mb_part,
            lg_acc + lg_part,
            lb_acc + lb_part,
            fg_acc + fg_part,
            fb_acc + fb_part,
            time_acc,
        )
        return (carry, (out_one, grad_media_in.astype(jnp.bfloat16), grad_latent_one))

    ff_local = up_weight.shape[1]
    vector_zero = jnp.zeros((width,), jnp.float32)
    start = (
        jnp.zeros((ff_local, width), jnp.float32),
        jnp.zeros((width, ff_local), jnp.float32),
        jnp.zeros((cols, width), jnp.float32),
        jnp.zeros((width, 2 * cols), jnp.float32),
        jnp.zeros((width, cols), jnp.float32),
        vector_zero,
        vector_zero,
        vector_zero,
        vector_zero,
        vector_zero,
        vector_zero,
        jnp.zeros((FRAMES_MAX, width), jnp.float32),
    )
    totals, stacked = lax.scan(item_step, start, (media_feats, latents, valid_tok, cotangent))
    (
        down_acc,
        up_acc,
        output_acc,
        keyval_acc,
        query_acc,
        mg_acc,
        mb_acc,
        lg_acc,
        lb_acc,
        fg_acc,
        fb_acc,
        time_acc,
    ) = totals
    out_latents, grad_media, grad_latents = stacked
    up_sum, down_sum, query_sum, keyval_sum, output_sum = (
        lax.psum_scatter(
            up_acc.astype(jnp.bfloat16), "wide", scatter_dimension=0, tiled=True
        ).astype(jnp.float32),
        lax.psum_scatter(
            down_acc.astype(jnp.bfloat16), "wide", scatter_dimension=1, tiled=True
        ).astype(jnp.float32),
        lax.psum_scatter(
            query_acc.astype(jnp.bfloat16), "wide", scatter_dimension=0, tiled=True
        ).astype(jnp.float32),
        lax.psum_scatter(
            keyval_acc.reshape(width, 2, cols).astype(jnp.bfloat16),
            "wide",
            scatter_dimension=0,
            tiled=True,
        ).astype(jnp.float32),
        lax.psum_scatter(
            output_acc.astype(jnp.bfloat16), "wide", scatter_dimension=1, tiled=True
        ).astype(jnp.float32),
    )
    mg_sum, mb_sum, lg_sum, lb_sum, fg_sum, fb_sum, time_sum = (
        lax.psum_scatter(mg_acc, ("wide", "narrow"), scatter_dimension=0, tiled=True),
        lax.psum_scatter(mb_acc, ("wide", "narrow"), scatter_dimension=0, tiled=True),
        lax.psum_scatter(lg_acc, ("wide", "narrow"), scatter_dimension=0, tiled=True),
        lax.psum_scatter(lb_acc, ("wide", "narrow"), scatter_dimension=0, tiled=True),
        lax.psum_scatter(fg_acc, ("wide", "narrow"), scatter_dimension=0, tiled=True),
        lax.psum_scatter(fb_acc, ("wide", "narrow"), scatter_dimension=0, tiled=True),
        lax.psum_scatter(time_acc, ("wide", "narrow"), scatter_dimension=1, tiled=True),
    )
    return (
        out_latents,
        grad_media,
        grad_latents,
        time_sum,
        mg_sum,
        mb_sum,
        lg_sum,
        lb_sum,
        fg_sum,
        fb_sum,
        query_sum,
        keyval_sum,
        output_sum,
        up_sum,
        down_sum,
    )


def solution(mesh):
    placed = (
        P("wide", "narrow", None),
        P("wide", "narrow", None),
        P("wide"),
        P("wide", None),
        P(),
        P(),
        P(),
        P(),
        P(),
        P(),
        P(),
        P("wide", "narrow"),
        P("wide", None, "narrow"),
        P("narrow", "wide"),
        P(None, "narrow"),
        P("narrow", None),
        P("wide", "narrow", None),
    )
    return jax.shard_map(
        body,
        mesh=mesh,
        in_specs=placed,
        out_specs=(
            P("wide", "narrow", None),
            P("wide", "narrow", None),
            P("wide", "narrow", None),
            P(None, ("wide", "narrow")),
            P(("wide", "narrow")),
            P(("wide", "narrow")),
            P(("wide", "narrow")),
            P(("wide", "narrow")),
            P(("wide", "narrow")),
            P(("wide", "narrow")),
            P("wide", "narrow"),
            P("wide", None, "narrow"),
            P("narrow", "wide"),
            P("wide", "narrow"),
            P("narrow", "wide"),
        ),
        check_vma=False,
    )
```

profile of v0, /device:TPU:0, one launch (start us, length us, event | category | flops | bytes accessed | tf_op | source)
XLA Modules:
  0.0 941.4 jit_solution(12498868731809088327)
XLA Ops:
  15.3 6.9 all_gather.36
  23.6 30.5 %all-gather.12.cloned.1.call-done = bf16[1536,384]{1,0:T(8,128)(2,1)} async-done(((bf16[192,384]{1,0:T(8,128)(2,1)}), bf16[1536,384]{1,0:T(8,128)(2,1)}) %all-gather.12.cloned.1.call-update) | async-done | bytes 1179664 | tf_op jit(solution)/shard_map/all_gather | solution.py:77
  55.8 51.6 %all-gather.10.cloned.1.call-done = bf16[1536,2,384]{2,0,1:T(8,128)(2,1)} async-done(((bf16[192,2,384]{2,0,1:T(8,128)(2,1)}), bf16[1536,2,384]{2,0,1:T(8,128)(2,1)}) %all-gather.10.cloned.1.call-update) | async-done | bytes 2359312 | tf_op jit(solution)/shard_map/all_gather | solution.py:78
  111.7 42.8 %all-gather.8.cloned.1.call-done = bf16[2048,1536]{1,0:T(8,128)(2,1)} async-done(((bf16[512,1536]{1,0:T(8,128)(2,1)}), bf16[2048,1536]{1,0:T(8,128)(2,1)}) %all-gather.8.cloned.1.call-update) | async-done | bytes 6291472 | tf_op jit(solution)/shard_map/while/body/eval_jaxpr/all_gather | solution.py:115
  181.3 16.3 %all-gather.14.cloned.1.call-done = bf16[384,1536]{0,1:T(8,128)(2,1)} async-done(((bf16[384,192]{0,1:T(8,128)(2,1)}), bf16[384,1536]{0,1:T(8,128)(2,1)}) %all-gather.14.cloned.1.call-update) | async-done | bytes 1179664 | tf_op jit(solution)/shard_map/all_gather | solution.py:79
  200.1 7.1 all-gather
  207.2 11.8 %reduce-scatter.11.cloned.1.call-done = bf16[16,1536]{1,0:T(8,128)(2,1)} async-done(((bf16[64,1536]{1,0:T(8,128)(2,1)}), bf16[16,1536]{1,0:T(8,128)(2,1)}) %reduce-scatter.11.cloned.1.call-update) | async-done | bytes 49168 | tf_op jit(solution)/shard_map/while/body/eval_jaxpr/reduce_scatter | solution.py:146
  221.9 5.6 all_gather.40
  241.6 19.1 %reduce-scatter.15.cloned.1.call-done = bf16[16,1536]{1,0:T(8,128)(2,1)} async-done(((bf16[64,1536]{1,0:T(8,128)(2,1)}), bf16[16,1536]{1,0:T(8,128)(2,1)}) %reduce-scatter.15.cloned.1.call-update) | async-done | bytes 49168 | tf_op jit(solution)/shard_map/while/body/eval_jaxpr/reduce_scatter | solution.py:173
  263.2 5.6 all_gather.42
  272.6 22.0 %psum.7 = f32[]{:T(128)} all-reduce(f32[]{:T(128)S(6)} %add.196), channel_id=1, replica_groups=mesh['wide'=8,'narrow'=4] {'wide'}, use_global_device_ids=true, to_apply=%region_14.15 | all-reduce | flops 1 | bytes 8 | tf_op jit(solution)/shard_map/psum | solution.py:73
  316.8 10.9 %convolution_convert_fusion.4 = bf16[1536,768]{0,1:T(8,128)(2,1)} fusion(bf16[2112,1536]{1,0:T(8,128)(2,1)} %copy-done.6, bf16[2112,384]{0,1:T(8,128)(2,1)S(1)} %bitcast.160, bf16[2112,384]{0,1:T(8,128)(2,1)S(1)} %bitcast.155), kind=kOutput, calls=%fused_computation.19 | convolution fusion | flops 4990500864 | bytes 12091392 | tf_op jit(solution)/shard_map/while/body/eval_jaxpr/kd,ke->de/dot_general | solution.py:215
  327.7 6.9 copy.135
  338.8 8.7 copy.126
  357.3 31.9 %all-to-all-done = bf16[2048,2,384]{2,1,0:T(2,128)(2,1)} async-done(((bf16[2048,2,384]{2,1,0:T(2,128)(2,1)}), bf16[2048,2,384]{2,1,0:T(2,128)(2,1)}, u32[]{:S(2)}, u32[]{:S(2)}) %all-to-all-start) | async-done | bytes 3145760 | tf_op jit(solution)/shard_map/while/body/eval_jaxpr/all_to_all | solution.py:230
  393.5 10.0 %multiply_reduce_fusion = (f32[1536]{0:T(1024)}, f32[512]{0:T(512)S(1)}, f32[512]{0:T(512)S(1)}, f32[1536]{0:T(1024)}, f32[512,1536]{1,0:T(8,128)S(1)}) fusion(f32[512,1536]{1,0:T(8,128)S(1)} %get-tuple-element.150, f32[512]{0:T(512)S(1)} %add_rsqrt_fusion, f32[512]{0:T(512)S(1)} %broadcast_multiply_fusion.2, f32[1536]{0:T(1024)S(1)} %copy-done.33, ...), kind=kOutput, calls=%fused_computation.23 | convolution fusion | flops 4838912000 | bytes 18900992 | tf_op jit(solution)/shard_map/while/body/eval_jaxpr/rsc,dsc->rd/dot_general | solution.py:233
  431.6 31.3 %reduce-scatter.17.cloned.1.call-done = bf16[192,384]{1,0:T(8,128)(2,1)} async-done(((bf16[1536,384]{1,0:T(8,128)(2,1)}), bf16[192,384]{1,0:T(8,128)(2,1)}) %reduce-scatter.17.cloned.1.call-update) | async-done | bytes 147472 | tf_op jit(solution)/shard_map/reduce_scatter | solution.py:306
  464.6 109.4 %all-reduce.11.cloned.1.call-done = bf16[1536,2,384]{2,1,0:T(2,128)(2,1)} async-done(((bf16[1536,2,384]{2,1,0:T(2,128)(2,1)}), bf16[1536,2,384]{2,1,0:T(2,128)(2,1)}) %all-reduce.11.cloned.1.call-update) | async-done | bytes 2359312
  576.0 6.2 convolution_bitcast_fusion.2
  582.3 29.8 %all-gather.18.cloned.1.call-done = bf16[1536,1536]{1,0:T(8,128)(2,1)} async-done(((bf16[1536,384]{1,0:T(8,128)(2,1)}), bf16[1536,1536]{1,0:T(8,128)(2,1)}) %all-gather.18.cloned.1.call-update) | async-done | bytes 4718608 | tf_op jit(solution)/shard_map/all_gather | solution.py:82
  616.0 40.1 %all-reduce.8 = (f32[1536]{0:T(1024)S(1)}, f32[1536]{0:T(1024)S(1)}, f32[1536]{0:T(1024)S(1)}, f32[1536]{0:T(1024)S(1)}, f32[1536]{0:T(1024)S(1)}, /*index=5*/f32[1536]{0:T(1024)S(1)}) all-reduce(f32[1536]{0:T(1024)S(1)} %copy-done.46, f32[1536]{0:T(1024)S(1)} %copy-done.47, ...), channel_id=7, replica_groups=mesh['wide'=8,'narrow'=4] {'wide','narrow'}, use_global_device_ids=true, to_apply=%region_23.24.clone | all-reduce | flops 9216 | bytes 73728
  661.2 74.4 %reduce-scatter.25.cloned.1.call-done = f32[48,8]{1,0:T(8,128)} async-done(((f32[1536,8]{1,0:T(8,128)}), f32[48,8]{1,0:T(8,128)}) %reduce-scatter.25.cloned.1.call-update) | async-done | bytes 1552
  737.0 96.9 %reduce-scatter.21.cloned.1.call-done = bf16[192,1536]{1,0:T(8,128)(2,1)} async-done(((bf16[1536,1536]{1,0:T(8,128)(2,1)}), bf16[192,1536]{1,0:T(8,128)(2,1)}) %reduce-scatter.21.cloned.1.call-update) | async-done | bytes 589840 | tf_op jit(solution)/shard_map/reduce_scatter | solution.py:300
  836.0 96.6 %reduce-scatter.23.cloned.1.call-done = bf16[1536,192]{0,1:T(8,128)(2,1)} async-done(((bf16[1536,1536]{0,1:T(8,128)(2,1)}), bf16[1536,192]{0,1:T(8,128)(2,1)}) %reduce-scatter.23.cloned.1.call-update) | async-done | bytes 589840 | tf_op jit(solution)/shard_map/reduce_scatter | solution.py:303
  (242 shorter events, 151.6 us)
Async XLA Ops:
  7.2 46.9 %all-gather.12.cloned.1.call-start = ((), (), s32[]{:S(2)}) async-start(), calls=%async_computation.12 | async-start | bytes 1327104 | tf_op jit(solution)/shard_map/all_gather | solution.py:77
  7.9 99.4 %all-gather.10.cloned.1.call-start = ((), (), s32[]{:S(2)}) async-start(), calls=%async_computation.11 | async-start | bytes 2654208 | tf_op jit(solution)/shard_map/all_gather | solution.py:78
  9.7 144.7 %all-gather.8.cloned.1.call-start = ((), (), s32[]{:S(2)}) async-start(), calls=%async_computation.10 | async-start | bytes 7864320 | tf_op jit(solution)/shard_map/while/body/eval_jaxpr/all_gather | solution.py:115
  14.2 183.4 %all-gather.14.cloned.1.call-start = ((), (), s32[]{:S(2)}) async-start(), calls=%async_computation.13 | async-start | bytes 1327104 | tf_op jit(solution)/shard_map/all_gather | solution.py:79
  14.8 204.2 %reduce-scatter.11.cloned.1.call-start = ((), (), s32[]{:S(2)}) async-start(), calls=%async_computation.14 | async-start | bytes 245760 | tf_op jit(solution)/shard_map/while/body/eval_jaxpr/reduce_scatter | solution.py:146
  23.5 149.4 %copy-start.54 = (pred[2112]{0:T(1024)(128)(4,1)}, pred[2112]{0:T(1024)(128)(4,1)S(1)}, u32[]{:S(2)}) copy-start(pred[2112]{0:T(1024)(128)(4,1)S(1)} %concatenate.18) | copy-start | bytes 6340
  55.8 117.2 %copy-start.27 = (bf16[64,4,96]{2,1,0:T(4,128)(2,1)}, bf16[64,4,96]{2,1,0:T(4,128)(2,1)S(1)}, u32[]{:S(2)}) copy-start(bf16[64,4,96]{2,1,0:T(4,128)(2,1)S(1)} %reshape.235) | copy-start | bytes 147460
  176.6 127.5 %copy-start.57 = (f32[4,64]{1,0:T(4,128)}, f32[4,64]{1,0:T(4,128)S(1)}, u32[]{:S(2)}) copy-start(f32[4,64]{1,0:T(4,128)S(1)} %get-tuple-element.151) | copy-start | bytes 3076
  200.1 60.6 %reduce-scatter.15.cloned.1.call-start = ((), (), s32[]{:S(2)}) async-start(), calls=%async_computation.16 | async-start | bytes 245760 | tf_op jit(solution)/shard_map/while/body/eval_jaxpr/reduce_scatter | solution.py:173
  240.8 152.7 %all-gather.16.cloned.1.call-start = ((), (), s32[]{:S(2)}) async-start(), calls=%async_computation.17 | async-start | bytes 11796480 | tf_op jit(solution)/shard_map/all_gather | solution.py:83
  241.5 188.5 %reduce-scatter.19.cloned.1.call-start = ((), (), s32[]{:S(2)}) async-start(), calls=%async_computation.20 | async-start | bytes 1327104 | tf_op jit(solution)/shard_map/reduce_scatter | solution.py:315
  271.9 191.0 %reduce-scatter.17.cloned.1.call-start = ((), (), s32[]{:S(2)}) async-start(), calls=%async_computation.19 | async-start | bytes 1327104 | tf_op jit(solution)/shard_map/reduce_scatter | solution.py:306
  311.9 262.1 %all-reduce.11.cloned.1.call-start = ((), (), s32[]{:S(2)}) async-start(), calls=%async_computation.24 | async-start | bytes 4718592
  334.6 277.5 %all-gather.18.cloned.1.call-start = ((), (), s32[]{:S(2)}) async-start(), calls=%async_computation.18 | async-start | bytes 5898240 | tf_op jit(solution)/shard_map/all_gather | solution.py:82
  347.6 41.7 %all-to-all-start = ((bf16[2048,2,384]{2,1,0:T(2,128)(2,1)}), bf16[2048,2,384]{2,1,0:T(2,128)(2,1)}, u32[]{:S(2)}, u32[]{:S(2)}) async-start(bf16[2048,2,384]{2,1,0:T(2,128)(2,1)} %copy.126), calls=%async_computation.3 | async-start | bytes 6291456 | tf_op jit(solution)/shard_map/while/body/eval_jaxpr/all_to_all | solution.py:230
  352.3 307.3 %reduce-scatter.13.cloned.1.call-start = ((), (), s32[]{:S(2)}) async-start(), calls=%async_computation.15 | async-start | bytes 245760 | tf_op jit(solution)/shard_map/while/body/eval_jaxpr/reduce_scatter | solution.py:158
  357.0 378.5 %reduce-scatter.25.cloned.1.call-start = ((), (), s32[]{:S(2)}) async-start(), calls=%async_computation.23 | async-start | bytes 811008
  409.3 424.6 %reduce-scatter.21.cloned.1.call-start = ((), (), s32[]{:S(2)}) async-start(), calls=%async_computation.21 | async-start | bytes 5308416 | tf_op jit(solution)/shard_map/reduce_scatter | solution.py:300
  412.9 519.8 %reduce-scatter.23.cloned.1.call-start = ((), (), s32[]{:S(2)}) async-start(), calls=%async_computation.22 | async-start | bytes 5308416 | tf_op jit(solution)/shard_map/reduce_scatter | solution.py:303
  421.3 8.6 all-to-all-start.1
  582.2 77.3 %copy-start.24 = (bf16[16,1536]{1,0:T(8,128)(2,1)S(1)}, bf16[16,1536]{1,0:T(8,128)(2,1)}, u32[]{:S(2)}) copy-start(bf16[16,1536]{1,0:T(8,128)(2,1)} %reduce-scatter.15.cloned.1.call-done) | copy-start | bytes 147460
  582.2 77.3 %copy-start.26 = (bf16[1,16,1536]{2,1,0:T(8,128)(2,1)S(1)}, bf16[1,16,1536]{2,1,0:T(8,128)(2,1)}, u32[]{:S(2)}) copy-start(bf16[1,16,1536]{2,1,0:T(8,128)(2,1)} %param.33) | copy-start | bytes 147460
  582.3 77.3 %copy-start.37 = (f32[16]{0:T(128)S(1)}, f32[16]{0:T(128)}, u32[]{:S(2)}) copy-start(f32[16]{0:T(128)} %copy-done.36) | copy-start | bytes 196
  612.1 322.7 %copy-start.1 = (bf16[8,1536]{1,0:T(8,128)(2,1)S(1)}, bf16[8,1536]{1,0:T(8,128)(2,1)}, u32[]{:S(2)}) copy-start(bf16[8,1536]{1,0:T(8,128)(2,1)} %param.21) | copy-start | bytes 73732
  (52 other events, 939.6 us)
Sparse Core Ops, SparseCore 0:
  10.2 43.8 all-gather.11
  56.8 50.4 all-gather.9
  109.5 44.8 all-gather.7
  156.5 41.1 all-gather.13
  200.5 18.4 reduce-scatter.10
  240.9 19.7 reduce-scatter.14
  262.3 64.0 all-gather.15
  330.4 64.8 reduce-scatter.18
  399.2 63.7 reduce-scatter.16
  466.4 107.5 all-reduce.10
  575.6 36.5 all-gather.17
  614.4 19.8 reduce-scatter.12
  639.4 96.1 reduce-scatter.24
  739.1 94.7 reduce-scatter.20
  837.3 95.2 reduce-scatter.22
where the time goes:
time: 944 us; the launch traced here: 941 us
  waiting for transfers between devices  649 us (69%)
  matrix products  95.8 us (10%)
  blocking collectives  87.2 us (9%)
  local copies, waits for them, and re-layouts  54.7 us (6%)
  other arithmetic  28.2 us (3%)
  between operations  17.4 us (2%)
    unnamed x17, waiting for transfers between devices  187 us
    reduce_scatter x1, waiting for transfers between devices, body(): lax.psum_scatter(up_acc.astype(jnp.bfloat16), 'wide', scatter_dimension=0...  96.9 us
    reduce_scatter x1, waiting for transfers between devices, body(): lax.psum_scatter(down_acc.astype(jnp.bfloat16), 'wide', scatter_dimension...  96.6 us
    all_gather x1, waiting for transfers between devices, body(): lax.all_gather(keyval_weight, 'wide', axis=0, tiled=True)  51.6 us
    all_gather x1, waiting for transfers between devices, item_step(): lax.all_gather(media_nf.astype(jnp.bfloat16), 'narrow', axis=0, tiled=True)  42.8 us
    unnamed x1, blocking collectives  40.1 us
    all_to_all x1, waiting for transfers between devices, item_step(): lax.all_to_all(media_pairs, 'narrow', split_axis=0, concat_axis=2, tiled=...  31.9 us
    reduce_scatter x1, waiting for transfers between devices, body(): lax.psum_scatter(query_acc.astype(jnp.bfloat16), 'wide', scatter_dimensio...  31.3 us
  transfers between devices with their start and end apart: 17, of which 14 were waited for; matrix products, arithmetic and copies ran while one was open for 16% of the time, Pallas kernels for 0%

commit v1 on v0

--- a/solution.py
+++ b/solution.py
@@ -11,6 +11,18 @@
 EPS = 1e-05
 ENT_COEF = 4.0
 HIGH = lax.Precision.HIGHEST
+
+
+def collect(x, axis, dim):
+    ways, here, step = (lax.axis_size(axis), lax.axis_index(axis), x.shape[dim])
+    line, have = (x, 1)
+    while have < ways:
+        line = jnp.concatenate(
+            [line, lax.ppermute(line, axis, [(d, (d - have) % ways) for d in range(ways)])],
+            axis=dim,
+        )
+        have = 2 * have
+    return jnp.roll(line, here * step, axis=dim)
 
 
 def norm_forward(values, norm_gain, norm_bias):
@@ -79,7 +91,7 @@
         lax.all_gather(output_weight, "wide", axis=1, tiled=True),
     )
     query_full, keyval_full = (
-        lax.all_gather(query_own, "narrow", axis=1, tiled=True),
+        collect(query_own, "narrow", 1),
         lax.all_gather(keyval_own, "narrow", axis=2, tiled=True),
     )
     keyval_flat = keyval_own.reshape(width, 2 * cols)

time: 944 us -> 913 us (0.967)
  waiting for transfers between devices: 649 us -> 593 us
  local copies, waits for them, and re-layouts: 54.7 us -> 67.1 us
    ppermute x0 -> x2, waiting for transfers between devices: none -> 62.8 us  [collect(): lax.ppermute(line, axis, [(d, (d - have) % ways) for d in range(ways)])]
    unnamed x17 -> x16, waiting for transfers between devices: 187 us -> 131 us
    reduce_scatter x1, waiting for transfers between devices: 31.3 us -> 0.01 us  [body(): lax.psum_scatter(query_acc.astype(jnp.bfloat16), 'wide', scatter_dimensio...]
    all_gather x1 -> x0, waiting for transfers between devices: 29.8 us -> none  [body(): lax.all_gather(query_own, 'narrow', axis=1, tiled=True)]
    unnamed x128 -> x139, local copies, waits for them, and re-layouts: 15.5 us -> 23.7 us
  transfers between devices with their start and end apart: 17 -> 18, of which waited for: 14 -> 14; matrix products, arithmetic and copies ran while one was open for 16% -> 19% of each run, Pallas kernels for 0% -> 0%
where the time goes in v1:
time: 913 us; the launch traced here: 902 us
  waiting for transfers between devices  593 us (65%)
  matrix products  96.4 us (11%)
  blocking collectives  87.4 us (10%)
  local copies, waits for them, and re-layouts  67.1 us (7%)
  other arithmetic  30.8 us (3%)
  between operations  17.5 us (2%)
  starting transfers between devices  10.5 us (1%)
    unnamed x16, waiting for transfers between devices  131 us
    reduce_scatter x1, waiting for transfers between devices, body(): lax.psum_scatter(down_acc.astype(jnp.bfloat16), 'wide', scatter_dimension...  97 us
    reduce_scatter x1, waiting for transfers between devices, body(): lax.psum_scatter(up_acc.astype(jnp.bfloat16), 'wide', scatter_dimension=0...  96.6 us
    ppermute x2, waiting for transfers between devices, collect(): lax.ppermute(line, axis, [(d, (d - have) % ways) for d in range(ways)])  62.8 us
    all_gather x1, waiting for transfers between devices, body(): lax.all_gather(keyval_weight, 'wide', axis=0, tiled=True)  51.6 us
    all_gather x1, waiting for transfers between devices, item_step(): lax.all_gather(media_nf.astype(jnp.bfloat16), 'narrow', axis=0, tiled=True)  42.7 us
    unnamed x1, blocking collectives  40.3 us
    all_to_all x1, waiting for transfers between devices, item_step(): lax.all_to_all(media_pairs, 'narrow', split_axis=0, concat_axis=2, tiled=...  31.7 us
  transfers between devices with their start and end apart: 18, of which 14 were waited for; matrix products, arithmetic and copies ran while one was open for 19% of the time, Pallas kernels for 0%

profile of v1, /device:TPU:0, one launch (start us, length us, event | category | flops | bytes accessed | tf_op | source)
XLA Modules:
  0.0 902.5 jit_solution(5582456053386781968)
XLA Ops:
  16.0 6.9 all_gather.33
  23.5 30.5 %all-gather.11.cloned.1.call-done = bf16[1536,384]{1,0:T(8,128)(2,1)} async-done(((bf16[192,384]{1,0:T(8,128)(2,1)}), bf16[1536,384]{1,0:T(8,128)(2,1)}) %all-gather.11.cloned.1.call-update) | async-done | bytes 1179664 | tf_op jit(solution)/shard_map/all_gather | solution.py:89
  55.8 51.6 %all-gather.9.cloned.1.call-done = bf16[1536,2,384]{2,0,1:T(8,128)(2,1)} async-done(((bf16[192,2,384]{2,0,1:T(8,128)(2,1)}), bf16[1536,2,384]{2,0,1:T(8,128)(2,1)}) %all-gather.9.cloned.1.call-update) | async-done | bytes 2359312 | tf_op jit(solution)/shard_map/all_gather | solution.py:90
  111.7 42.7 %all-gather.7.cloned.1.call-done = bf16[2048,1536]{1,0:T(8,128)(2,1)} async-done(((bf16[512,1536]{1,0:T(8,128)(2,1)}), bf16[2048,1536]{1,0:T(8,128)(2,1)}) %all-gather.7.cloned.1.call-update) | async-done | bytes 6291472 | tf_op jit(solution)/shard_map/while/body/eval_jaxpr/all_gather | solution.py:127
  181.4 16.5 %all-gather.13.cloned.1.call-done = bf16[384,1536]{0,1:T(8,128)(2,1)} async-done(((bf16[384,192]{0,1:T(8,128)(2,1)}), bf16[384,1536]{0,1:T(8,128)(2,1)}) %all-gather.13.cloned.1.call-update) | async-done | bytes 1179664 | tf_op jit(solution)/shard_map/all_gather | solution.py:91
  200.4 6.9 all-gather
  207.2 11.7 %reduce-scatter.11.cloned.1.call-done = bf16[16,1536]{1,0:T(8,128)(2,1)} async-done(((bf16[64,1536]{1,0:T(8,128)(2,1)}), bf16[16,1536]{1,0:T(8,128)(2,1)}) %reduce-scatter.11.cloned.1.call-update) | async-done | bytes 49168 | tf_op jit(solution)/shard_map/while/body/eval_jaxpr/reduce_scatter | solution.py:158
  221.9 5.6 all_gather.37
  241.6 19.1 %reduce-scatter.15.cloned.1.call-done = bf16[16,1536]{1,0:T(8,128)(2,1)} async-done(((bf16[64,1536]{1,0:T(8,128)(2,1)}), bf16[16,1536]{1,0:T(8,128)(2,1)}) %reduce-scatter.15.cloned.1.call-update) | async-done | bytes 49168 | tf_op jit(solution)/shard_map/while/body/eval_jaxpr/reduce_scatter | solution.py:185
  263.2 5.6 all_gather.39
  272.7 22.1 %psum.7 = f32[]{:T(128)} all-reduce(f32[]{:T(128)S(6)} %add.206), channel_id=1, replica_groups=mesh['wide'=8,'narrow'=4] {'wide'}, use_global_device_ids=true, to_apply=%region_14.15 | all-reduce | flops 1 | bytes 8 | tf_op jit(solution)/shard_map/psum | solution.py:85
  318.3 10.9 %convolution_convert_fusion.4 = bf16[1536,768]{0,1:T(8,128)(2,1)} fusion(bf16[2112,1536]{1,0:T(8,128)(2,1)} %copy-done.9, bf16[2112,384]{0,1:T(8,128)(2,1)S(1)} %bitcast.159, bf16[2112,384]{0,1:T(8,128)(2,1)S(1)} %bitcast.154), kind=kOutput, calls=%fused_computation.21 | convolution fusion | flops 4990500864 | bytes 12091392 | tf_op jit(solution)/shard_map/while/body/eval_jaxpr/kd,ke->de/dot_general | solution.py:227
  329.2 6.9 copy.135
  339.7 8.7 copy.126
  358.5 31.7 %all-to-all-done = bf16[2048,2,384]{2,1,0:T(2,128)(2,1)} async-done(((bf16[2048,2,384]{2,1,0:T(2,128)(2,1)}), bf16[2048,2,384]{2,1,0:T(2,128)(2,1)}, u32[]{:S(2)}, u32[]{:S(2)}) %all-to-all-start) | async-done | bytes 3145760 | tf_op jit(solution)/shard_map/while/body/eval_jaxpr/all_to_all | solution.py:242
  394.5 9.9 %multiply_reduce_fusion = (f32[1536]{0:T(1024)}, f32[512]{0:T(512)S(1)}, f32[512]{0:T(512)S(1)}, f32[1536]{0:T(1024)}, f32[512,1536]{1,0:T(8,128)S(1)}) fusion(f32[512,1536]{1,0:T(8,128)S(1)} %get-tuple-element.150, f32[512]{0:T(512)S(1)} %add_rsqrt_fusion, f32[512]{0:T(512)S(1)} %broadcast_multiply_fusion.2, f32[1536]{0:T(1024)S(1)} %copy-done.36, ...), kind=kOutput, calls=%fused_computation.25 | convolution fusion | flops 4838912000 | bytes 18900992 | tf_op jit(solution)/shard_map/while/body/eval_jaxpr/rsc,dsc->rd/dot_general | solution.py:245
  420.1 13.7 %collective-permute-done = bf16[1536,384]{1,0:T(8,128)(2,1)S(1)} collective-permute-done((bf16[1536,384]{1,0:T(8,128)(2,1)S(1)}, bf16[1536,384]{1,0:T(8,128)(2,1)S(1)}, u32[]{:S(2)}, u32[]{:S(2)}) %collective-permute-start) | collective-permute-done | bytes 1179680 | tf_op jit(solution)/shard_map/ppermute | solution.py:21
  440.5 49.1 %collective-permute-done.1 = bf16[1536,768]{1,0:T(8,128)(2,1)} collective-permute-done((bf16[1536,768]{1,0:T(8,128)(2,1)}, bf16[1536,768]{1,0:T(8,128)(2,1)}, u32[]{:S(2)}, u32[]{:S(2)}) %collective-permute-start.1) | collective-permute-done | bytes 2359328 | tf_op jit(solution)/shard_map/ppermute | solution.py:21
  509.7 63.9 %all-reduce.11.cloned.1.call-done = bf16[1536,2,384]{2,1,0:T(2,128)(2,1)} async-done(((bf16[1536,2,384]{2,1,0:T(2,128)(2,1)}), bf16[1536,2,384]{2,1,0:T(2,128)(2,1)}) %all-reduce.11.cloned.1.call-update) | async-done | bytes 2359312
  575.5 6.2 convolution_bitcast_fusion.2
  586.3 40.3 %all-reduce.8 = (f32[1536]{0:T(1024)S(1)}, f32[1536]{0:T(1024)S(1)}, f32[1536]{0:T(1024)S(1)}, f32[1536]{0:T(1024)S(1)}, f32[1536]{0:T(1024)S(1)}, /*index=5*/f32[1536]{0:T(1024)S(1)}) all-reduce(f32[1536]{0:T(1024)S(1)} %copy-done.49, f32[1536]{0:T(1024)S(1)} %copy-done.50, ...), channel_id=7, replica_groups=mesh['wide'=8,'narrow'=4] {'wide','narrow'}, use_global_device_ids=true, to_apply=%region_23.24.clone | all-reduce | flops 9216 | bytes 73728
  631.7 64.6 %reduce-scatter.25.cloned.1.call-done = f32[48,8]{1,0:T(8,128)} async-done(((f32[1536,8]{1,0:T(8,128)}), f32[48,8]{1,0:T(8,128)}) %reduce-scatter.25.cloned.1.call-update) | async-done | bytes 1552
  697.8 97.0 %reduce-scatter.23.cloned.1.call-done = bf16[1536,192]{0,1:T(8,128)(2,1)} async-done(((bf16[1536,1536]{0,1:T(8,128)(2,1)}), bf16[1536,192]{0,1:T(8,128)(2,1)}) %reduce-scatter.23.cloned.1.call-update) | async-done | bytes 589840 | tf_op jit(solution)/shard_map/reduce_scatter | solution.py:315
  796.9 96.6 %reduce-scatter.21.cloned.1.call-done = bf16[192,1536]{1,0:T(8,128)(2,1)} async-done(((bf16[1536,1536]{1,0:T(8,128)(2,1)}), bf16[192,1536]{1,0:T(8,128)(2,1)}) %reduce-scatter.21.cloned.1.call-update) | async-done | bytes 589840 | tf_op jit(solution)/shard_map/reduce_scatter | solution.py:312
  (256 shorter events, 166.1 us)
Async XLA Ops:
  7.2 46.9 %all-gather.11.cloned.1.call-start = ((), (), s32[]{:S(2)}) async-start(), calls=%async_computation.12 | async-start | bytes 1327104 | tf_op jit(solution)/shard_map/all_gather | solution.py:89
  7.9 99.4 %all-gather.9.cloned.1.call-start = ((), (), s32[]{:S(2)}) async-start(), calls=%async_computation.11 | async-start | bytes 2654208 | tf_op jit(solution)/shard_map/all_gather | solution.py:90
  9.7 144.7 %all-gather.7.cloned.1.call-start = ((), (), s32[]{:S(2)}) async-start(), calls=%async_computation.10 | async-start | bytes 7864320 | tf_op jit(solution)/shard_map/while/body/eval_jaxpr/all_gather | solution.py:127
  14.2 183.6 %all-gather.13.cloned.1.call-start = ((), (), s32[]{:S(2)}) async-start(), calls=%async_computation.13 | async-start | bytes 1327104 | tf_op jit(solution)/shard_map/all_gather | solution.py:91
  14.8 204.2 %reduce-scatter.11.cloned.1.call-start = ((), (), s32[]{:S(2)}) async-start(), calls=%async_computation.14 | async-start | bytes 245760 | tf_op jit(solution)/shard_map/while/body/eval_jaxpr/reduce_scatter | solution.py:158
  23.5 149.5 %copy-start.57 = (pred[2112]{0:T(1024)(128)(4,1)}, pred[2112]{0:T(1024)(128)(4,1)S(1)}, u32[]{:S(2)}) copy-start(pred[2112]{0:T(1024)(128)(4,1)S(1)} %concatenate.28) | copy-start | bytes 6340
  55.8 117.2 %copy-start.30 = (bf16[64,4,96]{2,1,0:T(4,128)(2,1)}, bf16[64,4,96]{2,1,0:T(4,128)(2,1)S(1)}, u32[]{:S(2)}) copy-start(bf16[64,4,96]{2,1,0:T(4,128)(2,1)S(1)} %reshape.235) | copy-start | bytes 147460
  176.6 129.0 %copy-start.60 = (f32[4,64]{1,0:T(4,128)}, f32[4,64]{1,0:T(4,128)S(1)}, u32[]{:S(2)}) copy-start(f32[4,64]{1,0:T(4,128)S(1)} %get-tuple-element.151) | copy-start | bytes 3076
  200.3 60.4 %reduce-scatter.15.cloned.1.call-start = ((), (), s32[]{:S(2)}) async-start(), calls=%async_computation.16 | async-start | bytes 245760 | tf_op jit(solution)/shard_map/while/body/eval_jaxpr/reduce_scatter | solution.py:185
  240.7 54.8 %copy-start.58 = (pred[2112]{0:T(1024)(128)(4,1)S(1)}, pred[2112]{0:T(1024)(128)(4,1)}, u32[]{:S(2)}) copy-start(pred[2112]{0:T(1024)(128)(4,1)} %copy-done.57) | copy-start | bytes 6340
  240.8 153.7 %all-gather.15.cloned.1.call-start = ((), (), s32[]{:S(2)}) async-start(), calls=%async_computation.17 | async-start | bytes 11796480 | tf_op jit(solution)/shard_map/all_gather | solution.py:95
  241.5 264.9 %reduce-scatter.19.cloned.1.call-start = ((), (), s32[]{:S(2)}) async-start(), calls=%async_computation.19 | async-start | bytes 1327104 | tf_op jit(solution)/shard_map/reduce_scatter | solution.py:327
  272.0 236.1 %reduce-scatter.17.cloned.1.call-start = ((), (), s32[]{:S(2)}) async-start(), calls=%async_computation.18 | async-start | bytes 1327104 | tf_op jit(solution)/shard_map/reduce_scatter | solution.py:318
  313.4 260.2 %all-reduce.11.cloned.1.call-start = ((), (), s32[]{:S(2)}) async-start(), calls=%async_computation.23 | async-start | bytes 4718592
  348.4 41.7 %all-to-all-start = ((bf16[2048,2,384]{2,1,0:T(2,128)(2,1)}), bf16[2048,2,384]{2,1,0:T(2,128)(2,1)}, u32[]{:S(2)}, u32[]{:S(2)}) async-start(bf16[2048,2,384]{2,1,0:T(2,128)(2,1)} %copy.126), calls=%async_computation.3 | async-start | bytes 6291456 | tf_op jit(solution)/shard_map/while/body/eval_jaxpr/all_to_all | solution.py:242
  353.2 276.9 %reduce-scatter.13.cloned.1.call-start = ((), (), s32[]{:S(2)}) async-start(), calls=%async_computation.15 | async-start | bytes 245760 | tf_op jit(solution)/shard_map/while/body/eval_jaxpr/reduce_scatter | solution.py:170
  357.9 338.4 %reduce-scatter.25.cloned.1.call-start = ((), (), s32[]{:S(2)}) async-start(), calls=%async_computation.22 | async-start | bytes 811008
  410.2 384.5 %reduce-scatter.23.cloned.1.call-start = ((), (), s32[]{:S(2)}) async-start(), calls=%async_computation.21 | async-start | bytes 5308416 | tf_op jit(solution)/shard_map/reduce_scatter | solution.py:315
  414.2 479.4 %reduce-scatter.21.cloned.1.call-start = ((), (), s32[]{:S(2)}) async-start(), calls=%async_computation.20 | async-start | bytes 5308416 | tf_op jit(solution)/shard_map/reduce_scatter | solution.py:312
  420.1 13.7 %collective-permute-start = (bf16[1536,384]{1,0:T(8,128)(2,1)S(1)}, bf16[1536,384]{1,0:T(8,128)(2,1)S(1)}, u32[]{:S(2)}, u32[]{:S(2)}) collective-permute-start(bf16[1536,384]{1,0:T(8,128)(2,1)S(1)} %copy-done.2), channel_id=1, source_target_pairs={{0,3},{1,0},{2,1},{3,2},{4,7},{5,4},{6,5},{7,6},{8,11},{9,8},{10,9... | collective-permute-start | bytes 3538952 | tf_op jit(solution)/shard_map/ppermute | solution.py:21
  435.6 54.0 %collective-permute-start.1 = (bf16[1536,768]{1,0:T(8,128)(2,1)}, bf16[1536,768]{1,0:T(8,128)(2,1)}, u32[]{:S(2)}, u32[]{:S(2)}) collective-permute-start(bf16[1536,768]{1,0:T(8,128)(2,1)} %pad_maximum_fusion.2), channel_id=1, source_target_pairs={{0,2},{1,3},{2,0},{3,1},{4,6},{5,7},{6,4},{7,5},{8,10},{9,11},{10,... | collective-permute-start | bytes 7077896 | tf_op jit(solution)/shard_map/ppermute | solution.py:21
  440.5 53.6 %copy-start.6 = (bf16[1536,384]{1,0:T(8,128)(2,1)S(1)}, bf16[1536,384]{1,0:T(8,128)(2,1)}, u32[]{:S(2)}) copy-start(bf16[1536,384]{1,0:T(8,128)(2,1)} %copy-done.5) | copy-start | bytes 3538948
  497.5 8.8 all-to-all-start.1
  581.9 313.9 %copy-start.1 = (bf16[8,1536]{1,0:T(8,128)(2,1)S(1)}, bf16[8,1536]{1,0:T(8,128)(2,1)}, u32[]{:S(2)}) copy-start(bf16[8,1536]{1,0:T(8,128)(2,1)} %param.21) | copy-start | bytes 73732
  (56 other events, 813.3 us)
Sparse Core Ops, SparseCore 0:
  10.2 43.8 all-gather.10
  56.8 50.4 all-gather.8
  109.5 44.8 all-gather.6
  156.5 41.3 all-gather.12
  200.7 18.2 reduce-scatter.10
  240.9 19.7 reduce-scatter.14
  262.3 64.1 all-gather.14
  329.8 64.7 reduce-scatter.18
  398.6 63.7 reduce-scatter.16
  465.8 107.6 all-reduce.10
  576.0 19.0 reduce-scatter.12
  600.0 96.3 reduce-scatter.24
  700.0 94.6 reduce-scatter.22
  798.2 95.2 reduce-scatter.20
